TPU v7x, 256 devices: a whole 4x4x8 slice. The times are simulated.
256 devices in a mesh: child: 2 (over y_hi), row: 32 (over z, y_lo, core), col: 4 (over x).
Axes of the slice: x: 4, y: 4 (y_hi: 2, y_lo: 2; y = y_hi * 2 + y_lo), z: 8, core: 2. Of those that a mesh axis runs over, the one named last changes fastest.
Arguments:
- front: bfloat16 [131072, 2048], P(('row', 'child'), 'col'), as said below
- left_factors: bfloat16 [2, 4, 64, 131072], P('child', 'col', None, 'row'), may hold values from -2.5 to 2.5
- right_factors: bfloat16 [2, 256, 64, 2048], P('child', 'row', None, 'col'), may hold values from -2.5 to 2.5
Outputs:
- panel_t: bfloat16 [2048, 131072], P('col', ('row', 'child'))
Inputs may be any that keep to these rules, and one draw needn't show every extreme that they name: The first 2048 rows of front make the symmetric part of the assembled diagonal block positive definite: its diagonal entries exceed the spectral norm of the rest of that part several times.
All inputs are finite; a program needn't handle non-finite values.
Results may differ from a plain program's by a relative error of at most 0.012.
Values may be sent and summed in bfloat16 or wider, within the bound.
No kernel may reach another device: no remote copies, remote signals or barrier semaphores. Data moves between devices by JAX's collectives and lax.ppermute only.
A program may use at most 128 MiB of HBM per device.

v0:
```python
import jax
import jax.numpy as jnp
from jax import lax
from jax.sharding import PartitionSpec as P

TILE = 512
RANK = 64
PW = 2048


def shortened(array):

    def short(part):
        return part.astype(jnp.bfloat16) if part.dtype == jnp.float32 else part

    return jax.tree.map(short, array)


def spread(value, axis, source):
    kept = jnp.where(lax.axis_index(axis) == source, value, 0).astype(value.dtype)
    return lax.psum(kept, axis)


def product_high(left, right):
    return jnp.dot(left, right, precision=lax.Precision.HIGHEST)


def inverse_transpose(top):
    blocks = PW // TILE
    identity = jnp.eye(TILE, dtype=jnp.float32)

    def tile_of(i, j):
        return top[i * TILE : (i + 1) * TILE, j * TILE : (j + 1) * TILE].astype(jnp.float32)

    def sym_tile(i, j):
        return 0.5 * (tile_of(i, j) + tile_of(j, i).T)

    lower = {}
    diag_inv = {}
    for j in range(blocks):
        accum = sym_tile(j, j)
        for k in range(j):
            accum = accum - product_high(lower[j, k], lower[j, k].T)
        lower[j, j] = jnp.linalg.cholesky(accum)
        diag_inv[j] = lax.linalg.triangular_solve(lower[j, j], identity, left_side=True, lower=True)
        for i in range(j + 1, blocks):
            accum = sym_tile(i, j)
            for k in range(j):
                accum = accum - product_high(lower[i, k], lower[j, k].T)
            lower[i, j] = product_high(accum, diag_inv[j].T)
    pieces = {}
    for i in range(blocks):
        pieces[i, i] = diag_inv[i]
    for i in range(blocks):
        for j in range(i):
            acc = jnp.zeros((TILE, TILE), jnp.float32)
            for k in range(j, i):
                acc = acc + product_high(lower[i, k], pieces[k, j])
            pieces[i, j] = -product_high(pieces[i, i], acc)
    zero_tile = jnp.zeros((TILE, TILE), jnp.bfloat16)
    row_list = [
        jnp.concatenate(
            [pieces[b, a].T.astype(jnp.bfloat16) if a <= b else zero_tile for b in range(blocks)],
            axis=1,
        )
        for a in range(blocks)
    ]
    return jnp.concatenate(row_list, axis=0)


def child_term(left_part, right_part):
    left_tiles = left_part.reshape(RANK, right_part.shape[0], TILE)
    result = jnp.einsum("rtk,trn->tkn", left_tiles, right_part, preferred_element_type=jnp.float32)
    return result.reshape(-1, TILE)


def shards(front, left_factors, right_factors):
    side = lax.axis_index("child")
    left_all = left_factors[0, 0]
    right_all = right_factors[0]
    update = lax.psum_scatter(
        child_term(left_all, right_all).astype(jnp.bfloat16),
        "child",
        scatter_dimension=0,
        tiled=True,
    ).astype(jnp.float32)
    panel_rows = (front.astype(jnp.float32) - update).astype(jnp.bfloat16)
    column = lax.axis_index("col")
    is_root = jnp.logical_and(side == 0, lax.axis_index("row") == 0)
    top = lax.all_gather(panel_rows[:PW], "col", axis=1, tiled=True)

    def select_block(matrix):
        return lax.dynamic_slice_in_dim(matrix, column * TILE, TILE, 0)

    empty_shape = (TILE, PW)
    local_block = lax.cond(
        is_root,
        lambda t: select_block(inverse_transpose(t)),
        lambda t: jnp.zeros(empty_shape, jnp.bfloat16),
        top,
    )
    inverse_block = jax.tree.map(
        lambda part, own: part.astype(own.dtype),
        jax.tree.map(lambda part: spread(part, ("child", "row"), 0), shortened(local_block)),
        local_block,
    )
    part = lax.slice_in_dim(inverse_block, 0, lax.axis_size("col") * TILE, axis=1)
    panel_t = lax.psum_scatter(
        lax.dot_general(
            part, panel_rows, (((0,), (1,)), ((), ())), preferred_element_type=jnp.float32
        ),
        "col",
        scatter_dimension=0,
        tiled=True,
    )
    return panel_t.astype(jnp.bfloat16)


def solution(mesh):
    in_specs = (
        P(("row", "child"), "col"),
        P("child", "col", None, "row"),
        P("child", "row", None, "col"),
    )
    out_specs = P("col", ("row", "child"))
    return jax.shard_map(shards, mesh=mesh, in_specs=in_specs, out_specs=out_specs, check_vma=False)
```

profile of v0, /device:TPU:1, one launch (start us, length us, event | category | flops | bytes accessed | tf_op | source)
XLA Modules:
  0.0 1288.6 jit_solution(6734739488787908376)
XLA Ops:
  6.5 0.0 copy-start
  6.5 0.0 reduce-scatter.3.cloned.1.call-start
  6.5 1.3 copy.31
  7.8 0.0 copy-done
  7.8 0.0 copy-start.46
  7.8 3.2 convolution_convert_fusion
  11.1 0.0 reduce-scatter.3.cloned.1.call-update
  11.1 0.0 all-gather.2.cloned.1.call-start
  11.1 64.8 %reduce-scatter.3.cloned.1.call-done = bf16[2048,512]{1,0:T(8,128)(2,1)} async-done(((bf16[4096,512]{1,0:T(8,128)(2,1)}), bf16[2048,512]{1,0:T(8,128)(2,1)}) %reduce-scatter.3.cloned.1.call-update) | async-done | bytes 2097168 | tf_op jit(solution)/shard_map/reduce_scatter | solution.py:81
  76.0 0.0 copy-done.46
  76.0 3.5 subtract_convert_fusion
  79.5 0.0 all-gather.2.cloned.1.call-update
  79.5 0.0 all-reduce.4.cloned.1.call-start
  79.5 85.1 %all-gather.2.cloned.1.call-done = bf16[2048,2048]{1,0:T(8,128)(2,1)} async-done(((bf16[2048,512]{1,0:T(8,128)(2,1)}), bf16[2048,2048]{1,0:T(8,128)(2,1)}) %all-gather.2.cloned.1.call-update) | async-done | bytes 8388624 | tf_op jit(solution)/shard_map/all_gather | solution.py:90
  164.7 1.5 conditional.1
  164.7 1.5 broadcast.134
  166.2 0.0 copy-start.35
  166.2 1.5 broadcast_select_fusion
  167.7 0.0 all-reduce.4.cloned.1.call-update
  167.7 0.0 reduce-scatter.5.cloned.1.call-start
  167.8 949.7 %all-reduce.4.cloned.1.call-done = bf16[512,2048]{0,1:T(8,128)(2,1)} async-done(((bf16[512,2048]{0,1:T(8,128)(2,1)}), bf16[512,2048]{0,1:T(8,128)(2,1)}) %all-reduce.4.cloned.1.call-update) | async-done | bytes 2097168 | tf_op jit(solution)/shard_map/psum | solution.py:21
  1117.5 0.0 copy-done.35
  1117.5 9.7 fusion.185
  1127.2 0.0 reduce-scatter.5.cloned.1.call-update
  1127.2 0.0 copy-start.1
  1127.2 151.0 %reduce-scatter.5.cloned.1.call-done = f32[512,2048]{1,0:T(8,128)} async-done(((f32[2048,2048]{1,0:T(8,128)}), f32[512,2048]{1,0:T(8,128)}) %reduce-scatter.5.cloned.1.call-update) | async-done | bytes 4194320 | tf_op jit(solution)/shard_map/reduce_scatter | solution.py:108
  1278.2 3.8 convert_element_type.129
  1282.1 0.0 copy-done.1
Async XLA Ops:
  6.5 1.3 copy-start
  6.5 69.4 %reduce-scatter.3.cloned.1.call-start = ((), (), s32[]{:S(2)}) async-start(), calls=%async_computation.2 | async-start | bytes 6291456 | tf_op jit(solution)/shard_map/reduce_scatter | solution.py:81
  7.8 68.1 %copy-start.46 = (bf16[2048,512]{1,0:T(8,128)(2,1)S(1)}, bf16[2048,512]{1,0:T(8,128)(2,1)}, u32[]{:S(2)}) copy-start(bf16[2048,512]{1,0:T(8,128)(2,1)} %param.8) | copy-start | bytes 6291460
  11.1 153.6 %all-gather.2.cloned.1.call-start = ((), (), s32[]{:S(2)}) async-start(), calls=%async_computation.3 | async-start | bytes 10485760 | tf_op jit(solution)/shard_map/all_gather | solution.py:90
  79.5 1038.0 %all-reduce.4.cloned.1.call-start = ((), (), s32[]{:S(2)}) async-start(), calls=%async_computation.4 | async-start | bytes 4194304 | tf_op jit(solution)/shard_map/psum | solution.py:21
  166.2 951.3 %copy-start.35 = (bf16[2048,512]{1,0:T(8,128)(2,1)S(1)}, bf16[2048,512]{1,0:T(8,128)(2,1)}, u32[]{:S(2)}) copy-start(bf16[2048,512]{1,0:T(8,128)(2,1)} %subtract_convert_fusion) | copy-start | bytes 6291460
  167.7 1110.5 %reduce-scatter.5.cloned.1.call-start = ((), (), s32[]{:S(2)}) async-start(), calls=%async_computation.5 | async-start | bytes 20971520 | tf_op jit(solution)/shard_map/reduce_scatter | solution.py:108
  1127.2 154.8 %copy-start.1 = (bf16[1,8,64,512]{3,2,1,0:T(8,128)(2,1)S(1)}, bf16[1,8,64,512]{3,2,1,0:T(8,128)(2,1)}, u32[]{:S(2)}) copy-start(bf16[1,8,64,512]{3,2,1,0:T(8,128)(2,1)} %param.10) | copy-start | bytes 1572868
Sparse Core Ops, SparseCore 0:
  11.2 64.6 reduce-scatter.2
  79.6 85.0 all-gather.1
  168.5 948.9 all-reduce.3
  1127.3 150.8 reduce-scatter.4
where the time goes:
time: 1290 us
  waiting for transfers between devices  1250 us (97%)
  between operations  13.2 us (1%)
  matrix products  12.9 us (1%)
    psum x1, waiting for transfers between devices, spread(): return lax.psum(kept, axis)  950 us
    reduce_scatter x1, waiting for transfers between devices, shards(): lax.psum_scatter(lax.dot_general(part, panel_rows, (((0,), (1,)), ((), ()...  151 us
    all_gather x1, waiting for transfers between devices, shards(): top = lax.all_gather(panel_rows[:PW], 'col', axis=1, tiled=True)  85.1 us
    reduce_scatter x1, waiting for transfers between devices, shards(): lax.psum_scatter(child_term(left_all, right_all).astype(jnp.bfloat16), 'c...  64.8 us
  transfers between devices with their start and end apart: 4, of which 4 were waited for; matrix products, arithmetic and copies ran while one was open for 0% of the time, Pallas kernels for 0%

commit v1 on v0

--- a/solution.py
+++ b/solution.py
@@ -6,6 +6,24 @@
 TILE = 512
 RANK = 64
 PW = 2048
+
+
+def collect(value, axis, dim):
+    ways, here, step = (lax.axis_size(axis), lax.axis_index(axis), value.shape[dim])
+    lengths = [n * ways if d == dim else n for d, n in enumerate(value.shape)]
+    full = lax.dynamic_update_slice_in_dim(
+        jnp.zeros(lengths, value.dtype), value, here * step, axis=dim
+    )
+    going_up = going_down = value
+    for far in range(1, ways // 2 + 1):
+        going_up = lax.ppermute(going_up, axis, [(d, (d + 1) % ways) for d in range(ways)])
+        full = lax.dynamic_update_slice_in_dim(full, going_up, (here - far) % ways * step, axis=dim)
+        if 2 * far < ways:
+            going_down = lax.ppermute(going_down, axis, [(d, (d - 1) % ways) for d in range(ways)])
+            full = lax.dynamic_update_slice_in_dim(
+                full, going_down, (here + far) % ways * step, axis=dim
+            )
+    return full
 
 
 def shortened(array):
@@ -87,7 +105,7 @@
     panel_rows = (front.astype(jnp.float32) - update).astype(jnp.bfloat16)
     column = lax.axis_index("col")
     is_root = jnp.logical_and(side == 0, lax.axis_index("row") == 0)
-    top = lax.all_gather(panel_rows[:PW], "col", axis=1, tiled=True)
+    top = collect(panel_rows[:PW], "col", 1)
 
     def select_block(matrix):
         return lax.dynamic_slice_in_dim(matrix, column * TILE, TILE, 0)

time: 1290 us -> 1340 us (1.039)
  waiting for transfers between devices: 1250 us -> 1290 us
    ppermute x0 -> x3, waiting for transfers between devices: none -> 92 us  [the longest x2 92 us: collect(): lax.ppermute(going_up, axis, [(d, (d + 1) % ways) for d in range(ways)])]
    all_gather x1 -> x0, waiting for transfers between devices: 85.1 us -> none  [shards(): top = lax.all_gather(panel_rows[:PW], 'col', axis=1, tiled=True)]
    psum x1, waiting for transfers between devices: 950 us -> 982 us  [spread(): return lax.psum(kept, axis)]
  transfers between devices with their start and end apart: 4 -> 6, of which waited for: 4 -> 5; matrix products, arithmetic and copies ran while one was open for 0% -> 0% of each run, Pallas kernels for 0% -> 0%
where the time goes in v1:
time: 1340 us; the launch traced here: 1330 us
  waiting for transfers between devices  1290 us (96%)
  matrix products  15.7 us (1%)
    psum x1, waiting for transfers between devices, spread(): return lax.psum(kept, axis)  982 us
    reduce_scatter x1, waiting for transfers between devices, shards(): lax.psum_scatter(lax.dot_general(part, panel_rows, (((0,), (1,)), ((), ()...  151 us
    ppermute x2, waiting for transfers between devices, collect(): lax.ppermute(going_up, axis, [(d, (d + 1) % ways) for d in range(ways)])  92 us
    reduce_scatter x1, waiting for transfers between devices, shards(): lax.psum_scatter(child_term(left_all, right_all).astype(jnp.bfloat16), 'c...  64.8 us
  transfers between devices with their start and end apart: 6, of which 5 were waited for; matrix products, arithmetic and copies ran while one was open for 0% of the time, Pallas kernels for 0%

profile of v1, /device:TPU:1, one launch (start us, length us, event | category | flops | bytes accessed | tf_op | source)
XLA Modules:
  0.0 1331.7 jit_solution(7496000228711934007)
XLA Ops:
  6.5 0.0 copy-start
  6.5 0.0 reduce-scatter.3.cloned.1.call-start
  6.5 1.3 copy.88
  7.8 0.0 copy-done
  7.8 0.0 copy-start.41
  7.8 3.2 convolution_convert_fusion
  11.1 0.0 reduce-scatter.3.cloned.1.call-update
  11.1 0.0 all-reduce.4.cloned.1.call-start
  11.1 64.8 %reduce-scatter.3.cloned.1.call-done = bf16[2048,512]{1,0:T(8,128)(2,1)} async-done(((bf16[4096,512]{1,0:T(8,128)(2,1)}), bf16[2048,512]{1,0:T(8,128)(2,1)}) %reduce-scatter.3.cloned.1.call-update) | async-done | bytes 2097168 | tf_op jit(solution)/shard_map/reduce_scatter | solution.py:99
  76.0 0.0 copy-done.41
  76.0 3.5 subtract_convert_fusion
  79.5 1.2 collective-permute-start
  80.7 1.5 collective-permute-start.1
  82.1 45.2 %collective-permute-done = bf16[2048,512]{1,0:T(8,128)(2,1)S(1)} collective-permute-done((bf16[2048,512]{1,0:T(8,128)(2,1)}, bf16[2048,512]{1,0:T(8,128)(2,1)S(1)}, u32[]{:S(2)}, u32[]{:S(2)}) %collective-permute-start) | collective-permute-done | bytes 2097184 | tf_op jit(solution)/shard_map/ppermute | solution.py:19
  127.3 0.1 collective-permute-start.2
  127.5 0.0 collective-permute-done.1
  127.5 46.7 %collective-permute-done.2 = bf16[2048,512]{1,0:T(8,128)(2,1)} collective-permute-done((bf16[2048,512]{1,0:T(8,128)(2,1)S(1)}, bf16[2048,512]{1,0:T(8,128)(2,1)}, u32[]{:S(2)}, u32[]{:S(2)}) %collective-permute-start.2) | collective-permute-done | bytes 2097184 | tf_op jit(solution)/shard_map/ppermute | solution.py:19
  174.2 0.4 conditional.1
  174.2 0.1 broadcast.146
  174.6 1.5 broadcast_select_fusion
  176.1 0.0 all-reduce.4.cloned.1.call-update
  176.1 0.0 reduce-scatter.5.cloned.1.call-start
  176.2 981.7 %all-reduce.4.cloned.1.call-done = bf16[512,2048]{0,1:T(8,128)(2,1)} async-done(((bf16[512,2048]{0,1:T(8,128)(2,1)}), bf16[512,2048]{0,1:T(8,128)(2,1)}) %all-reduce.4.cloned.1.call-update) | async-done | bytes 2097168 | tf_op jit(solution)/shard_map/psum | solution.py:39
  1157.8 12.5 fusion.181
  1170.3 0.0 reduce-scatter.5.cloned.1.call-update
  1170.3 0.0 copy-start.1
  1170.3 151.0 %reduce-scatter.5.cloned.1.call-done = f32[512,2048]{1,0:T(8,128)} async-done(((f32[2048,2048]{1,0:T(8,128)}), f32[512,2048]{1,0:T(8,128)}) %reduce-scatter.5.cloned.1.call-update) | async-done | bytes 4194320 | tf_op jit(solution)/shard_map/reduce_scatter | solution.py:126
  1321.3 3.8 convert_element_type.210
  1325.2 0.0 copy-done.1
Async XLA Ops:
  6.5 1.3 copy-start
  6.5 69.4 %reduce-scatter.3.cloned.1.call-start = ((), (), s32[]{:S(2)}) async-start(), calls=%async_computation.2 | async-start | bytes 6291456 | tf_op jit(solution)/shard_map/reduce_scatter | solution.py:99
  7.8 68.1 %copy-start.41 = (bf16[2048,512]{1,0:T(8,128)(2,1)S(1)}, bf16[2048,512]{1,0:T(8,128)(2,1)}, u32[]{:S(2)}) copy-start(bf16[2048,512]{1,0:T(8,128)(2,1)} %param.8) | copy-start | bytes 6291460
  11.1 1146.7 %all-reduce.4.cloned.1.call-start = ((), (), s32[]{:S(2)}) async-start(), calls=%async_computation.3 | async-start | bytes 4194304 | tf_op jit(solution)/shard_map/psum | solution.py:39
  79.5 47.9 %collective-permute-start = (bf16[2048,512]{1,0:T(8,128)(2,1)}, bf16[2048,512]{1,0:T(8,128)(2,1)S(1)}, u32[]{:S(2)}, u32[]{:S(2)}) collective-permute-start(bf16[2048,512]{1,0:T(8,128)(2,1)} %subtract_convert_fusion), channel_id=1, source_target_pairs={{0,1},{1,2},{2,3},{3,0},{4,5},{5,6},{6,7},{7,4},{8,9},{9,10},{10,1... | collective-permute-start | bytes 6291464 | tf_op jit(solution)/shard_map/ppermute | solution.py:19
  80.7 46.8 %collective-permute-start.1 = (bf16[2048,512]{1,0:T(8,128)(2,1)}, bf16[2048,512]{1,0:T(8,128)(2,1)}, u32[]{:S(2)}, u32[]{:S(2)}) collective-permute-start(bf16[2048,512]{1,0:T(8,128)(2,1)} %subtract_convert_fusion), channel_id=1, source_target_pairs={{0,3},{1,0},{2,1},{3,2},{4,7},{5,4},{6,5},{7,6},{8,11},{9,8},{10,9... | collective-permute-start | bytes 6291464 | tf_op jit(solution)/shard_map/ppermute | solution.py:22
  127.3 46.9 %collective-permute-start.2 = (bf16[2048,512]{1,0:T(8,128)(2,1)S(1)}, bf16[2048,512]{1,0:T(8,128)(2,1)}, u32[]{:S(2)}, u32[]{:S(2)}) collective-permute-start(bf16[2048,512]{1,0:T(8,128)(2,1)S(1)} %collective-permute-done), channel_id=1, source_target_pairs={{0,1},{1,2},{2,3},{3,0},{4,5},{5,6},{6,7},{7,4},{8,9},{9,10},{10,1... | collective-permute-start | bytes 6291464 | tf_op jit(solution)/shard_map/ppermute | solution.py:19
  176.1 1145.2 %reduce-scatter.5.cloned.1.call-start = ((), (), s32[]{:S(2)}) async-start(), calls=%async_computation.4 | async-start | bytes 20971520 | tf_op jit(solution)/shard_map/reduce_scatter | solution.py:126
  1170.3 154.8 %copy-start.1 = (bf16[1,8,64,512]{3,2,1,0:T(8,128)(2,1)S(1)}, bf16[1,8,64,512]{3,2,1,0:T(8,128)(2,1)}, u32[]{:S(2)}) copy-start(bf16[1,8,64,512]{3,2,1,0:T(8,128)(2,1)} %param.10) | copy-start | bytes 1572868
Sparse Core Ops, SparseCore 0:
  11.2 64.6 reduce-scatter.2
  176.2 981.5 all-reduce.3
  1170.5 150.8 reduce-scatter.4
